TPU v7x, 256 devices: a whole 4x4x8 slice. The times are simulated.
256 devices in a mesh: pair: 16 (over z, core), red: 16 (over x, y).
Axes of the slice: x: 4, y: 4, z: 8, core: 2. Of those that a mesh axis runs over, the one named last changes fastest.
Arguments:
- three_center: bfloat16 [2304, 256, 256], P('pair', 'red'), may hold values from -0.375 to 0.375
- occ_src: int32 [256, 16], P('red'), may hold values from 0 to 15, as said below
- occ_block: int32 [256, 16], P('red'), may hold values from 0 to 31
- occ_blocks: bfloat16 [512, 256], P('red'), may hold values from -0.375 to 0.375
- virt_block: int32 [16, 16, 1], P('red'), may hold values from 0 to 31, as said below
- virt_blocks: bfloat16 [16, 32, 256], P('red', 'pair'), may hold values from -1.5 to 1.5
Outputs:
- chi: float32 [2304, 2304], P('pair', 'red')
Inputs may be any that keep to these rules, and one draw needn't show every extreme that they name: `occ_src`: the 16 entries of a row are distinct. `virt_block`: every block listed for tile t of a red group lies from (t) * 2 to (t) * 2 + 1.
All inputs are finite; a program needn't handle non-finite values.
Results may differ from a plain program's by a relative error of at most 0.0041.
Values may be sent and summed in bfloat16 or wider, within the bound.
A program may use at most 128 MiB of HBM per device.

v0:
```python
import jax
import jax.numpy as jnp
from jax import lax
from jax.sharding import PartitionSpec as P

BLK = 16
TPD = 1


def occupied(three_center, occ_src, occ_block, occ_blocks):
    aux_rows, ntiles, area = three_center.shape
    nblocks = occ_blocks.shape[0]
    block_hot = (
        occ_block[:, :, None] == jnp.arange(nblocks, dtype=jnp.int32)[None, None, :]
    ).astype(jnp.bfloat16)
    picked = jnp.einsum(
        "tsb,bk->tsk", block_hot, occ_blocks, preferred_element_type=jnp.float32
    ).astype(jnp.bfloat16)
    source_hot = (occ_src[:, :, None] == jnp.arange(ntiles, dtype=jnp.int32)[None, None, :]).astype(
        jnp.bfloat16
    )
    mixing = jnp.einsum(
        "tsk,tsa->tka", source_hot, picked, preferred_element_type=jnp.float32
    ).astype(jnp.bfloat16)
    mixing = mixing.reshape(ntiles, ntiles, BLK, BLK)
    blocks = three_center.reshape(aux_rows, ntiles, BLK, BLK)
    half = jnp.einsum("tkml,pkln->ptmn", mixing, blocks, preferred_element_type=jnp.float32)
    return half.reshape(aux_rows, ntiles, area).astype(jnp.bfloat16)


def virtual(half, listed, blocks):
    aux_rows, ntiles, area = half.shape
    owners = listed.shape[0]
    nblocks = blocks.shape[0]
    block_hot = (listed[..., None] == jnp.arange(nblocks, dtype=jnp.int32)).astype(jnp.bfloat16)
    picked = jnp.einsum(
        "oijb,bk->oijk", block_hot, blocks, preferred_element_type=jnp.float32
    ).astype(jnp.bfloat16)
    picked = picked.reshape(owners, TPD, TPD, BLK, BLK)
    grouped = half.reshape(aux_rows, owners, TPD, BLK, BLK)
    kernel = jnp.einsum("pojml,oijln->poimn", grouped, picked, preferred_element_type=jnp.float32)
    return kernel.reshape(aux_rows, ntiles, area).astype(jnp.bfloat16)


def shards(three_center, occ_src, occ_block, occ_blocks, virt_block, virt_blocks):
    aux_rows, ntiles, area = three_center.shape
    half = occupied(three_center, occ_src, occ_block, occ_blocks)
    own_blocks = virt_blocks[0]
    listed = virt_block[0]
    all_blocks = lax.all_gather(own_blocks, "pair", axis=0, tiled=True)
    kernel = virtual(half, listed.reshape(ntiles // TPD, TPD, TPD), all_blocks)
    flat_tiles = three_center.reshape(aux_rows, ntiles * area)
    piece = lax.all_gather(kernel, "pair", axis=0, tiled=True)
    flat_piece = piece.reshape(piece.shape[0], ntiles * area)
    partial_value = lax.dot_general(
        flat_tiles, flat_piece, (((1,), (1,)), ((), ())), preferred_element_type=jnp.float32
    )
    return lax.psum_scatter(partial_value, "red", scatter_dimension=1, tiled=True)


def solution(mesh):
    placed = (
        P("pair", "red", None),
        P("red", None),
        P("red", None),
        P("red", None),
        P("red", None, None),
        P("red", "pair", None),
    )
    return jax.shard_map(
        shards, mesh=mesh, in_specs=placed, out_specs=P("pair", "red"), check_vma=False
    )
```

profile of v0, /device:TPU:32, one launch (start us, length us, event | category | flops | bytes accessed | tf_op | source)
XLA Modules:
  0.0 243.4 jit_solution(1345893647742258906)
XLA Ops:
  6.5 0.0 copy-start
  6.5 0.0 copy-start.1
  6.5 0.0 all-gather.3.cloned.1.call-start
  6.5 0.8 copy.21
  7.3 17.9 %all-gather = bf16[1,32,256]{2,0,1:T(2,128)(2,1)S(1)} all-gather(bf16[1,2,256]{2,0,1:T(2,128)(2,1)S(1)} %copy.21), channel_id=2, replica_groups=mesh['pair'=16,'red'=16] {'pair'}, dimensions={1}, use_global_device_ids=true | all-gather | bytes 17408 | tf_op jit(solution)/shard_map/all_gather | solution.py:50
  25.2 0.8 convolution_convert_fusion.2
  26.1 0.1 reshape.42
  26.2 0.0 copy-done
  26.2 1.1 convolution_convert_fusion
  27.3 1.7 reshape.47
  29.0 0.0 copy-done.1
  29.0 1.2 copy.22
  30.2 3.4 %fusion.7 = bf16[144,16,16,16]{0,2,3,1:T(8,128)(2,1)S(1)} fusion(bf16[144,16,16,16]{0,3,2,1:T(8,128)(2,1)S(1)} %bitcast.43, bf16[16,16,16,16,1]{3,2,1,0,4:T(8,128)(2,1)} %reshape.47), kind=kOutput, calls=%fused_computation.7 | convolution fusion | flops 302579712 | bytes 2490368 | tf_op jit(solution)/shard_map/tkml,pkln->ptmn/dot_general | solution.py:27
  33.5 2.2 fusion.4
  35.7 3.7 %copy.26 = bf16[144,16,256]{2,0,1:T(8,128)(2,1)} copy(bf16[144,16,256]{0,2,1:T(8,128)(2,1)} %bitcast.44) | data formatting | bytes 2359296 | tf_op jit(solution)/shard_map/convert_element_type | solution.py:42
  39.4 0.0 all-gather.3.cloned.1.call-update
  39.4 0.0 reduce-scatter.4.cloned.1.call-start
  39.5 103.4 %all-gather.3.cloned.1.call-done = bf16[2304,16,256]{2,0,1:T(8,128)(2,1)} async-done(((bf16[144,16,256]{2,0,1:T(8,128)(2,1)}), bf16[2304,16,256]{2,0,1:T(8,128)(2,1)}) %all-gather.3.cloned.1.call-update) | async-done | bytes 18874384 | tf_op jit(solution)/shard_map/all_gather | solution.py:53
  142.8 9.5 %convolution_bitcast_fusion = f32[144,2304]{1,0:T(8,128)S(1)} fusion(bf16[2304,16,256]{2,0,1:T(8,128)(2,1)} %all-gather.3.cloned.1.call-done, bf16[144,16,256]{0,2,1:T(8,128)(2,1)S(1)} %copy.22), kind=kOutput, calls=%fused_computation.1 | convolution fusion | flops 2717908992 | bytes 21381120 | tf_op jit(solution)/shard_map/dot_general | solution.py:55
  152.3 1.9 copy.33
  154.2 0.0 reduce-scatter.4.cloned.1.call-update
  154.3 80.6 %reduce-scatter.4.cloned.1.call-done = f32[144,144]{1,0:T(8,128)} async-done(((f32[2304,144]{1,0:T(8,128)}), f32[144,144]{1,0:T(8,128)}) %reduce-scatter.4.cloned.1.call-update) | async-done | bytes 82960
  234.9 1.7 copy.34
Async XLA Ops:
  6.5 19.6 %copy-start = (bf16[32,256]{1,0:T(8,128)(2,1)S(1)}, bf16[32,256]{1,0:T(8,128)(2,1)}, u32[]{:S(2)}) copy-start(bf16[32,256]{1,0:T(8,128)(2,1)} %param.9) | copy-start | bytes 49156
  6.5 22.4 %copy-start.1 = (bf16[144,16,256]{2,1,0:T(8,128)(2,1)S(1)}, bf16[144,16,256]{2,1,0:T(8,128)(2,1)}, u32[]{:S(2)}) copy-start(bf16[144,16,256]{2,1,0:T(8,128)(2,1)} %param.6) | copy-start | bytes 3538948
  6.5 136.3 %all-gather.3.cloned.1.call-start = ((), (), s32[]{:S(2)}) async-start(), calls=%async_computation.1 | async-start | bytes 20054016 | tf_op jit(solution)/shard_map/all_gather | solution.py:53
  39.4 195.4 %reduce-scatter.4.cloned.1.call-start = ((), (), s32[]{:S(2)}) async-start(), calls=%async_computation.2 | async-start | bytes 2506752
Sparse Core Ops, SparseCore 0:
  39.6 103.2 all-gather.2
  154.4 80.4 reduce-scatter.3
where the time goes:
time: 244 us; the launch traced here: 243 us
  waiting for transfers between devices  184 us (75%)
  blocking collectives  17.9 us (7%)
  matrix products  17 us (7%)
  between operations  13.4 us (5%)
  local copies, waits for them, and re-layouts  11 us (5%)
    all_gather x1, waiting for transfers between devices, shards(): piece = lax.all_gather(kernel, 'pair', axis=0, tiled=True)  103 us
    unnamed x3, waiting for transfers between devices  80.6 us
    all_gather x1, blocking collectives, shards(): all_blocks = lax.all_gather(own_blocks, 'pair', axis=0, tiled=True)  17.9 us
    dot_general x1, matrix products, shards(): lax.dot_general(flat_tiles, flat_piece, (((1,), (1,)), ((), ())), preferr...  9.48 us
    unnamed x8, local copies, waits for them, and re-layouts  5.55 us
  transfers between devices with their start and end apart: 2, of which 2 were waited for; matrix products, arithmetic and copies ran while one was open for 0% of the time, Pallas kernels for 0%

commit v1 on v0

--- a/solution.py
+++ b/solution.py
@@ -50,7 +50,9 @@
     all_blocks = lax.all_gather(own_blocks, "pair", axis=0, tiled=True)
     kernel = virtual(half, listed.reshape(ntiles // TPD, TPD, TPD), all_blocks)
     flat_tiles = three_center.reshape(aux_rows, ntiles * area)
-    piece = lax.all_gather(kernel, "pair", axis=0, tiled=True)
+    piece = jnp.concatenate(
+        lax.all_to_all(jnp.stack([kernel] * lax.axis_size("pair")), "pair", 0, 0), axis=0
+    )
     flat_piece = piece.reshape(piece.shape[0], ntiles * area)
     partial_value = lax.dot_general(
         flat_tiles, flat_piece, (((1,), (1,)), ((), ())), preferred_element_type=jnp.float32

time: 244 us -> 566 us (2.32)
  waiting for transfers between devices: 184 us -> 488 us
  local copies, waits for them, and re-layouts: 11 us -> 28.4 us
  starting transfers between devices: 0.04 us -> 7.38 us
  matrix products: 17 us -> 9.9 us
    all_to_all x0 -> x1, waiting for transfers between devices: none -> 407 us  [shards(): lax.all_to_all(jnp.stack([kernel] * lax.axis_size('pair')), 'pair', 0, 0)]
    all_gather x1 -> x0, waiting for transfers between devices: 103 us -> none  [shards(): piece = lax.all_gather(kernel, 'pair', axis=0, tiled=True)]
    unnamed x8 -> x20, local copies, waits for them, and re-layouts: 5.55 us -> 19.7 us
    all_to_all x0 -> x1, starting transfers between devices: none -> 7.34 us  [shards(): lax.all_to_all(jnp.stack([kernel] * lax.axis_size('pair')), 'pair', 0, 0)]
    another operation x1 -> x2, local copies, waits for them, and re-layouts: 0.1 us -> 6.75 us  [the longest x1 6.64 us: shards(): jnp.stack([kernel] * lax.axis_size('pair'))]
    unnamed x3 -> x2, waiting for transfers between devices: 80.6 us -> 81.3 us
where the time goes in v1:
time: 566 us
  waiting for transfers between devices  488 us (86%)
  local copies, waits for them, and re-layouts  28.4 us (5%)
  blocking collectives  17.9 us (3%)
  between operations  13.5 us (2%)
  matrix products  9.9 us (2%)
  starting transfers between devices  7.38 us (1%)
    all_to_all x1, waiting for transfers between devices, shards(): lax.all_to_all(jnp.stack([kernel] * lax.axis_size('pair')), 'pair', 0, 0)  407 us
    unnamed x2, waiting for transfers between devices  81.3 us
    unnamed x20, local copies, waits for them, and re-layouts  19.7 us
    all_gather x1, blocking collectives, shards(): all_blocks = lax.all_gather(own_blocks, 'pair', axis=0, tiled=True)  17.9 us
  transfers between devices with their start and end apart: 2, of which 2 were waited for; matrix products, arithmetic and copies ran while one was open for 0% of the time, Pallas kernels for 0%

profile of v1, /device:TPU:32, one launch (start us, length us, event | category | flops | bytes accessed | tf_op | source)
XLA Modules:
  0.0 565.6 jit_solution(9826902022894653531)
XLA Ops:
  6.5 2.7 copy.19
  9.3 0.0 copy-done
  9.3 0.0 copy-done.4
  9.3 0.0 copy-done.3
  9.3 0.4 convolution_convert_fusion
  9.7 0.7 reshape.52
  10.4 17.9 %all-gather = bf16[1,32,256]{2,0,1:T(2,128)(2,1)S(1)} all-gather(bf16[1,2,256]{2,0,1:T(2,128)(2,1)S(1)} %copy.18), channel_id=2, replica_groups=mesh['pair'=16,'red'=16] {'pair'}, dimensions={1}, use_global_device_ids=true | all-gather | bytes 17408 | tf_op jit(solution)/shard_map/all_gather | solution.py:50
  28.4 0.2 convolution_convert_fusion.2
  28.6 0.1 reshape.46
  28.7 2.2 fusion.7
  30.8 0.8 fusion.4
  31.7 1.3 copy.23
  33.0 6.6 %stack.2 = bf16[16,144,16,256]{3,2,1,0:T(8,128)(2,1)} broadcast(bf16[144,16,256]{2,1,0:T(8,128)(2,1)S(1)} %copy.23), dimensions={1,2,3} | broadcast | bytes 20054016 | tf_op jit(solution)/shard_map/stack | solution.py:54
  39.6 7.3 %all-to-all-start = ((bf16[16,144,16,256]{3,2,1,0:T(8,128)(2,1)}), bf16[16,144,16,256]{3,2,1,0:T(8,128)(2,1)}, u32[]{:S(2)}, u32[]{:S(2)}) async-start(bf16[16,144,16,256]{3,2,1,0:T(8,128)(2,1)} %stack.2), calls=%async_computation | async-start | bytes 37748736 | tf_op jit(solution)/shard_map/all_to_all | solution.py:54
  47.0 0.0 reduce-scatter.4.cloned.1.call-start
  47.0 0.5 copy.33
  47.5 407.2 %all-to-all-done = bf16[16,144,16,256]{3,2,1,0:T(8,128)(2,1)} async-done(((bf16[16,144,16,256]{3,2,1,0:T(8,128)(2,1)}), bf16[16,144,16,256]{3,2,1,0:T(8,128)(2,1)}, u32[]{:S(2)}, u32[]{:S(2)}) %all-to-all-start) | async-done | bytes 18874400 | tf_op jit(solution)/shard_map/all_to_all | solution.py:54
  454.7 12.8 %copy.32 = bf16[288,8,16,256]{3,1,2,0:T(8,128)(2,1)S(1)} copy(bf16[288,8,16,256]{3,2,1,0:T(8,128)(2,1)} %bitcast.21) | data formatting | bytes 37748736
  467.6 6.3 %convolution_bitcast_fusion = f32[144,2304]{1,0:T(8,128)S(1)} fusion(bf16[2304,4096]{1,0:T(8,128)(2,1)S(1)} %bitcast.45, bf16[144,4096]{1,0:T(8,128)(2,1)S(1)} %bitcast.50), kind=kOutput, calls=%fused_computation.1 | convolution fusion | flops 2717908992 | bytes 21381120 | tf_op jit(solution)/shard_map/dot_general | solution.py:57
  473.9 0.0 copy-start.1
  473.9 1.9 copy.29
  475.8 0.0 reduce-scatter.4.cloned.1.call-update
  475.8 81.3 %reduce-scatter.4.cloned.1.call-done = f32[144,144]{1,0:T(8,128)} async-done(((f32[2304,144]{1,0:T(8,128)}), f32[144,144]{1,0:T(8,128)}) %reduce-scatter.4.cloned.1.call-update) | async-done | bytes 82960
  557.1 1.7 copy.30
  (11 shorter events, 0.0 us)
Async XLA Ops:
  6.5 2.8 copy-start
  6.5 2.8 copy-start.4
  6.5 2.8 copy-start.3
  6.5 3.9 copy-start.5
  6.5 21.8 %copy-start.6 = (s32[1,16,1]{1,2,0:T(1,128)S(1)}, s32[1,16,1]{1,2,0:T(1,128)}, u32[]{:S(2)}) copy-start(s32[1,16,1]{1,2,0:T(1,128)} %param.10) | copy-start | bytes 196
  39.6 7.4 %copy-start.2 = (bf16[144,16,256]{2,1,0:T(8,128)(2,1)S(1)}, bf16[144,16,256]{2,1,0:T(8,128)(2,1)}, u32[]{:S(2)}) copy-start(bf16[144,16,256]{2,1,0:T(8,128)(2,1)} %param.6) | copy-start | bytes 3538948
  39.6 415.1 %all-to-all-start = ((bf16[16,144,16,256]{3,2,1,0:T(8,128)(2,1)}), bf16[16,144,16,256]{3,2,1,0:T(8,128)(2,1)}, u32[]{:S(2)}, u32[]{:S(2)}) async-start(bf16[16,144,16,256]{3,2,1,0:T(8,128)(2,1)} %stack.2), calls=%async_computation | async-start | bytes 37748736 | tf_op jit(solution)/shard_map/all_to_all | solution.py:54
  47.0 510.1 %reduce-scatter.4.cloned.1.call-start = ((), (), s32[]{:S(2)}) async-start(), calls=%async_computation.2 | async-start | bytes 2506752
  473.9 84.9 %copy-start.1 = (bf16[32,256]{1,0:T(8,128)(2,1)S(1)}, bf16[32,256]{1,0:T(8,128)(2,1)}, u32[]{:S(2)}) copy-start(bf16[32,256]{1,0:T(8,128)(2,1)} %param.9) | copy-start | bytes 49156
Sparse Core Ops, SparseCore 0:
  476.0 81.0 reduce-scatter.3
